TPU v7x, 512 devices: a whole 4x8x8 slice. The times are simulated.
512 devices in a mesh: sta: 8 (over z_hi, x), tm: 64 (over y, z_lo, core).
Axes of the slice: x: 4, y: 8, z: 8 (z_hi: 2, z_lo: 4; z = z_hi * 4 + z_lo), core: 2. Of those that a mesh axis runs over, the one named last changes fastest.
Arguments:
- record: bfloat16 [96, 49152], P('sta', 'tm')
- templates: bfloat16 [64, 96, 512], P('tm', 'sta'), may hold values from -6 to 6
- shifts: int32 [96], P('sta'), may hold values from 0 to 255, as said below
- live_mask: int32 [96], P('sta'), may hold values 0 or 1
- plan: int32 [64], replicated, may hold values from 0 to 63, each once
Outputs:
- stacks: float32 [64, 49152], P('sta', 'tm')
Inputs may be any that keep to these rules, and one draw needn't show every extreme that they name: `shifts`: some channel has the shift 256 - 1. `plan`: each bank slot appears once.
All inputs are finite; a program needn't handle non-finite values. No bound on the sum of `live_mask` on one device may be relied on, other than what follows from the above.
Results may differ from a plain program's by a relative error of at most 0.0003.
Values may be sent and summed in bfloat16 or wider, within the bound.
A program may use at most 64 MiB of HBM per device.

v0:
```python
import math

import jax
import jax.numpy as jnp
from jax import lax
from jax.sharding import PartitionSpec as P

CHANNELS = 96


def passed_along(shard, axis, by):
    count = lax.axis_size(axis)
    pairs = [(i, i + by) for i in range(count) if 0 <= i + by < count]
    return lax.ppermute(shard, axis, pairs)


def hankel_rows(signal, taps_len, span_len):
    length = signal.shape[0]
    copies = jnp.tile(signal, taps_len + 1)
    skewed = copies[: taps_len * (length + 1)].reshape(taps_len, length + 1)
    return skewed[:, :span_len]


def correlate(panels_in, aligned, live_vals, taps_len, span_len, group_cap):
    tmpl_rows, chan_count, _ = panels_in.shape
    group_size = math.gcd(chan_count, group_cap)
    overall = math.sqrt(taps_len / CHANNELS)
    norm_vals = jnp.sqrt(jnp.sum(jnp.square(panels_in.astype(jnp.float32)), axis=2) + 1e-06)
    weights = live_vals[None, :] * overall / norm_vals
    in_pos = lax.broadcasted_iota(jnp.int32, (span_len + taps_len, span_len), 0)
    out_pos = lax.broadcasted_iota(jnp.int32, (span_len + taps_len, span_len), 1)
    band_ones = ((in_pos >= out_pos) & (in_pos < out_pos + taps_len)).astype(jnp.float32)

    def add_group(group_idx, running):
        first_chan = group_idx * group_size
        panel_part = lax.dynamic_slice_in_dim(panels_in, first_chan, group_size, 1)
        window = lax.dynamic_slice_in_dim(aligned, first_chan, group_size, 0)
        stacked = jax.vmap(lambda signal_row: hankel_rows(signal_row, taps_len, span_len))(window)
        products = jnp.einsum(
            "rgl,glt->rgt", panel_part, stacked, preferred_element_type=jnp.float32
        )
        squares = jnp.square(window.astype(jnp.float32))
        energy = jnp.dot(squares, band_ones, precision=lax.Precision.HIGHEST)
        weighting = lax.dynamic_slice_in_dim(weights, first_chan, group_size, 1)
        scaled = products * weighting[:, :, None] * lax.rsqrt(energy + 1e-06)[None, :, :]
        return running + jnp.sum(scaled, axis=1)

    start_val = jnp.zeros((tmpl_rows, span_len), jnp.float32)
    return lax.fori_loop(0, chan_count // group_size, add_group, start_val)


def per_device(record, templates, shifts, live_mask, plan):
    taps_len = templates.shape[2]
    span_len = record.shape[1]
    live_vals = live_mask.astype(jnp.float32)
    rim_part = passed_along(record, "tm", -1)
    extended = jnp.concatenate([record, rim_part], axis=1)
    aligned = jax.vmap(
        lambda signal_row, lag_val: lax.dynamic_slice_in_dim(
            signal_row, lag_val, span_len + taps_len
        )
    )(extended, shifts)
    bank_all = lax.all_gather(templates, "tm", axis=0, tiled=True)
    ordered = jnp.take(bank_all, plan, axis=0)
    partial_value = correlate(ordered, aligned, live_vals, taps_len, span_len, 8)
    return lax.psum_scatter(partial_value, "sta", scatter_dimension=0, tiled=True)


def solution(mesh):
    placed = (P("sta", "tm"), P("tm", "sta", None), P("sta"), P("sta"), P())
    return jax.shard_map(
        per_device, mesh=mesh, in_specs=placed, out_specs=P("sta", "tm"), check_vma=False
    )
```

profile of v0, /device:TPU:1, one launch (start us, length us, event | category | flops | bytes accessed | tf_op | source)
XLA Modules:
  0.0 317.1 jit_solution(1732965342201204)
XLA Ops:
  6.5 8.9 %collective-permute-start = (bf16[12,768]{1,0:T(8,128)(2,1)}, bf16[12,768]{1,0:T(8,128)(2,1)S(1)}, u32[]{:S(2)}, u32[]{:S(2)}) collective-permute-start(bf16[12,768]{1,0:T(8,128)(2,1)} %param.7), channel_id=1, source_target_pairs={{1,0},{2,1},{3,2},{4,3},{5,4},{6,5},{7,6},{8,7},{9,8},{10,9},{11,1... | collective-permute-start | bytes 55304 | tf_op jit(solution)/shard_map/ppermute | solution.py:14
  15.4 0.7 compare_select_fusion
  16.1 0.7 compare_and_fusion
  16.7 0.7 fusion.30
  17.4 80.2 %all_gather.3 = bf16[64,12,512]{2,1,0:T(8,128)(2,1)S(1)} all-gather(bf16[1,12,512]{2,1,0:T(8,128)(2,1)} %param.8), channel_id=1, replica_groups=mesh['sta'=8,'tm'=64] {'tm'}, dimensions={0}, use_global_device_ids=true | all-gather | bytes 798720 | tf_op jit(solution)/shard_map/all_gather | solution.py:63
  97.6 0.7 convert_multiply_fusion
  98.3 0.6 gather_fusion
  98.9 0.5 multiply_reduce_fusion
  99.6 25.1 %while.15 = (s32[]{:T(128)}, bf16[12,1536]{1,0:T(8,128)(2,1)S(1)}, s32[12,2]{0,1:T(2,128)S(1)}, bf16[12,1280]{1,0:T(8,128)(2,1)S(1)}, s32[]{:T(128)}, /*index=5*/s32[]{:T(128)}) while((s32[]{:T(128)}, bf16[12,1536]{1,0:T(8,128)(2,1)S(1)}, s32[12,2]{0,1:T(2,128)S(1)}, bf16[12,1280]{1,0:T(8,128)(2,1)S(1)}, s32[]{:T(128)}, /*index=5*/s32[]{:T(128)}) %tuple.49), condition=%wide.while_cond, body=%wide.while_body.sunk | while | flops 2 | bytes 10361 | solution.py:59
  99.6 0.1 constant_dynamic-slice_fusion.8
  99.7 0.6 fusion.39
  100.2 1.4 dynamic-slice.7
  101.7 0.1 constant_dynamic-slice_fusion.8
  101.8 0.6 fusion.39
  102.3 1.4 dynamic-slice.7
  103.8 0.6 fusion.39
  104.4 1.4 dynamic-slice.7
  105.9 0.6 fusion.39
  106.5 1.4 dynamic-slice.7
  108.0 0.1 constant_dynamic-slice_fusion.8
  108.0 0.6 fusion.39
  108.6 1.4 dynamic-slice.7
  110.1 0.6 fusion.39
  110.7 1.4 dynamic-slice.7
  112.2 0.6 fusion.39
  112.8 1.4 dynamic-slice.7
  114.2 0.1 constant_dynamic-slice_fusion.8
  114.3 0.6 fusion.39
  114.9 1.4 dynamic-slice.7
  116.4 0.6 fusion.39
  117.0 1.4 dynamic-slice.7
  118.5 0.6 fusion.39
  119.0 1.4 dynamic-slice.7
  120.6 0.6 fusion.39
  121.1 1.4 dynamic-slice.7
  122.6 0.6 fusion.39
  123.2 1.4 dynamic-slice.7
  124.7 98.8 %while.16 = (s32[]{:T(128)}, f32[64,768]{1,0:T(8,128)S(1)}, bf16[12,1280]{1,0:T(8,128)(2,1)S(1)}, bf16[64,12,512]{2,1,0:T(8,128)(2,1)S(1)}, f32[64,12]{0,1:T(8,1...) while((s32[]{:T(128)}, f32[64,768]{1,0:T(8,128)S(1)}, ...), condition=%wide.region_3.4_spmd.clone, body=%wide.region_1.3_spmd.clone.sunk | while | flops 253096960 | bytes 52031664 | solution.py:49
  124.7 0.3 broadcast_bitcast_fusion.2
  125.1 2.0 copy.16
  127.1 4.0 %slice.49 = bf16[4,655872]{1,0:T(4,128)(2,1)} slice(bf16[4,656640]{1,0:T(4,128)(2,1)S(1)} %bitcast.25), slice={[0:4], [0:655872]} | slice | bytes 10493952 | tf_op jit(solution)/shard_map/while/body/eval_jaxpr/vmap()/slice | solution.py:20
  131.1 6.8 %reshape.53 = bf16[2623488]{0:T(1024)(128)(2,1)} reshape(bf16[4,655872]{1,0:T(4,128)(2,1)} %slice.49) | data formatting | bytes 10493952 | tf_op jit(solution)/shard_map/while
  137.9 14.9 %reshape.54 = bf16[4,512,1281]{2,1,0:T(8,128)(2,1)} reshape(bf16[2623488]{0:T(1024)(128)(2,1)} %reshape.53) | data formatting | bytes 10493952 | tf_op jit(solution)/shard_map/while/body/eval_jaxpr/vmap()/reshape | solution.py:20
  152.8 2.0 fusion.44
  154.8 0.1 constant_dynamic-slice_fusion.11
  155.0 2.6 fusion.45
  157.6 0.3 broadcast_bitcast_fusion.2
  158.0 2.0 copy.16
  160.0 4.0 %slice.49 = bf16[4,655872]{1,0:T(4,128)(2,1)} slice(bf16[4,656640]{1,0:T(4,128)(2,1)S(1)} %bitcast.25), slice={[0:4], [0:655872]} | slice | bytes 10493952 | tf_op jit(solution)/shard_map/while/body/eval_jaxpr/vmap()/slice | solution.py:20
  164.1 6.8 %reshape.53 = bf16[2623488]{0:T(1024)(128)(2,1)} reshape(bf16[4,655872]{1,0:T(4,128)(2,1)} %slice.49) | data formatting | bytes 10493952 | tf_op jit(solution)/shard_map/while
  170.9 14.9 %reshape.54 = bf16[4,512,1281]{2,1,0:T(8,128)(2,1)} reshape(bf16[2623488]{0:T(1024)(128)(2,1)} %reshape.53) | data formatting | bytes 10493952 | tf_op jit(solution)/shard_map/while/body/eval_jaxpr/vmap()/reshape | solution.py:20
  185.8 2.0 fusion.44
  187.8 0.1 constant_dynamic-slice_fusion.11
  187.9 2.6 fusion.45
  190.6 0.3 broadcast_bitcast_fusion.2
  190.9 2.0 copy.16
  193.0 4.0 %slice.49 = bf16[4,655872]{1,0:T(4,128)(2,1)} slice(bf16[4,656640]{1,0:T(4,128)(2,1)S(1)} %bitcast.25), slice={[0:4], [0:655872]} | slice | bytes 10493952 | tf_op jit(solution)/shard_map/while/body/eval_jaxpr/vmap()/slice | solution.py:20
  197.0 6.8 %reshape.53 = bf16[2623488]{0:T(1024)(128)(2,1)} reshape(bf16[4,655872]{1,0:T(4,128)(2,1)} %slice.49) | data formatting | bytes 10493952 | tf_op jit(solution)/shard_map/while
  203.8 14.9 %reshape.54 = bf16[4,512,1281]{2,1,0:T(8,128)(2,1)} reshape(bf16[2623488]{0:T(1024)(128)(2,1)} %reshape.53) | data formatting | bytes 10493952 | tf_op jit(solution)/shard_map/while/body/eval_jaxpr/vmap()/reshape | solution.py:20
  218.7 2.0 fusion.44
  220.7 0.1 constant_dynamic-slice_fusion.11
  220.9 2.6 fusion.45
  223.5 0.7 copy-done
  224.2 86.1 %reduce-scatter.2.cloned.1.call-done = f32[8,768]{1,0:T(8,128)} async-done(((f32[64,768]{1,0:T(8,128)}), f32[8,768]{1,0:T(8,128)}) %reduce-scatter.2.cloned.1.call-update) | async-done | bytes 24592 | tf_op jit(solution)/shard_map/reduce_scatter | solution.py:66
  (44 shorter events, 1.7 us)
Async XLA Ops:
  6.5 93.0 %copy-start.1 = (bf16[12,768]{1,0:T(8,128)(2,1)S(1)}, bf16[12,768]{1,0:T(8,128)(2,1)}, u32[]{:S(2)}) copy-start(bf16[12,768]{1,0:T(8,128)(2,1)} %param.7) | copy-start | bytes 55300
  6.5 303.7 %reduce-scatter.2.cloned.1.call-start = ((), (), s32[]{:S(2)}) async-start(), calls=%async_computation.1 | async-start | bytes 221184 | tf_op jit(solution)/shard_map/reduce_scatter | solution.py:66
  6.5 93.0 %collective-permute-start = (bf16[12,768]{1,0:T(8,128)(2,1)}, bf16[12,768]{1,0:T(8,128)(2,1)S(1)}, u32[]{:S(2)}, u32[]{:S(2)}) collective-permute-start(bf16[12,768]{1,0:T(8,128)(2,1)} %param.7), channel_id=1, source_target_pairs={{1,0},{2,1},{3,2},{4,3},{5,4},{6,5},{7,6},{8,7},{9,8},{10,9},{11,1... | collective-permute-start | bytes 55304 | tf_op jit(solution)/shard_map/ppermute | solution.py:14
  223.5 0.7 copy-start
Sparse Core Ops, SparseCore 0:
  224.3 85.9 reduce-scatter.1
where the time goes:
time: 319 us; the launch traced here: 317 us
  local copies, waits for them, and re-layouts  111 us (35%)
  waiting for transfers between devices  86.1 us (27%)
  blocking collectives  80.2 us (25%)
  matrix products  13.6 us (4%)
  between operations  13.5 us (4%)
  starting transfers between devices  8.87 us (3%)
  other arithmetic  3.33 us (1%)
    reduce_scatter x1, waiting for transfers between devices, per_device(): lax.psum_scatter(partial_value, 'sta', scatter_dimension=0, tiled=True)  86.1 us
    all_gather x1, blocking collectives, per_device(): bank_all = lax.all_gather(templates, 'tm', axis=0, tiled=True)  80.2 us
    reshape x3, local copies, waits for them, and re-layouts, hankel_rows(): skewed = copies[:taps_len * (length + 1)].reshape(taps_len, length + 1)  44.7 us
    while x9, local copies, waits for them, and re-layouts  27.6 us
    gather x48, local copies, waits for them, and re-layouts  24.8 us
    slice x3, local copies, waits for them, and re-layouts, hankel_rows(): skewed = copies[:taps_len * (length + 1)].reshape(taps_len, length + 1)  12 us
    ppermute x1, starting transfers between devices, passed_along(): return lax.ppermute(shard, axis, pairs)  8.87 us
    dot_general x3, matrix products, add_group(): jnp.einsum('rgl,glt->rgt', panel_part, stacked, preferred_element_type=jn...  7.72 us
  transfers between devices with their start and end apart: 2, of which 1 were waited for; matrix products, arithmetic and copies ran while one was open for 1% of the time, Pallas kernels for 0%

commit v1 on v0

v1 whole, which is shorter than its diff:
```python
import functools
import math

import jax
import jax.numpy as jnp
from jax import lax
from jax.experimental import pallas as pl
from jax.experimental.pallas import tpu as pltpu
from jax.sharding import PartitionSpec as P

CHANNELS = 96
ZRUN = 4
ZHALVES = 2
MESH = pl.DeviceIdType.MESH


def shifted_left(value, by):
    width = value.shape[1]
    if by % width == 0:
        return value
    return pltpu.roll(value, width - by, 1)


def stack_kernel(
    sizes,
    record,
    templates,
    shifts,
    live,
    plan,
    out,
    rec_buf,
    halo,
    bank,
    wave,
    hankel,
    gain,
    aligned,
    total,
    row_recv,
    far_send,
    far_recv,
    shift_s,
    live_s,
    plan_s,
    load_sem,
    halo_sem,
    send_sem,
    recv_sem,
    pair_send,
    pair_recv,
    row_ssem,
    row_rsem,
    far_sem,
):
    rows_y, cols_x, chans, span, taps = sizes
    count = rows_y * ZRUN * 2
    ext = 2 * span
    reach = span + taps
    sta = lax.axis_index("sta")
    me = lax.axis_index("tm")
    core = me % 2
    at_z = (me // 2) % ZRUN
    at_y = me // (2 * ZRUN)
    at_x = sta % cols_x
    half = sta // cols_x

    def slot(y, z, c):
        return (y * ZRUN + z) * 2 + c

    after, before = (me + 1) % count, (me + count - 1) % count
    partner = slot(at_y, at_z, 1 - core)
    y_peers = [slot((at_y + d) % rows_y, at_z, core) for d in range(1, rows_y)]
    z_peers = [slot(at_y, (at_z + d) % ZRUN, core) for d in range(1, ZRUN)]
    x_peers = [half * cols_x + (at_x + d) % cols_x for d in range(1, cols_x)]
    far_peer = (1 - half) * cols_x + at_x
    outer = jnp.where(core == 0, before, after)

    loads = [
        pltpu.make_async_copy(record, rec_buf, load_sem.at[0]),
        pltpu.make_async_copy(templates.at[0], bank.at[me], load_sem.at[1]),
        pltpu.make_async_copy(shifts, shift_s, load_sem.at[2]),
        pltpu.make_async_copy(live, live_s, load_sem.at[3]),
        pltpu.make_async_copy(plan, plan_s, load_sem.at[4]),
    ]
    for load in loads:
        load.start()

    barrier = pltpu.get_barrier_semaphore()
    met = [{"tm": p} for p in y_peers + z_peers + [partner, outer]]
    met += [{"sta": p} for p in x_peers + [far_peer]]
    for peer in met:
        pl.semaphore_signal(barrier, inc=1, device_id=peer, device_id_type=MESH)
    pl.semaphore_wait(barrier, len(met))

    def piece_copy(src, owner, target, sem_at):
        return pltpu.make_async_remote_copy(
            src_ref=src,
            dst_ref=bank.at[owner],
            send_sem=send_sem.at[sem_at],
            recv_sem=recv_sem.at[owner],
            device_id={"tm": target},
            device_id_type=MESH,
        )

    def pair_copy(src, owner, sem_at):
        return pltpu.make_async_remote_copy(
            src_ref=src,
            dst_ref=bank.at[owner],
            send_sem=pair_send.at[sem_at],
            recv_sem=pair_recv.at[owner],
            device_id={"tm": partner},
            device_id_type=MESH,
        )

    own = templates.at[0]
    z_steps = [1, 3, 2]
    y_steps = [4, 3, 5, 2, 6, 1, 7] if rows_y == 8 else list(range(1, rows_y))
    firsts = []
    for at, d in enumerate(z_steps):
        firsts.append(piece_copy(own, me, slot(at_y, (at_z + d) % ZRUN, core), at))
    for at, d in enumerate(y_steps):
        firsts.append(piece_copy(own, me, slot((at_y + d) % rows_y, at_z, core), len(z_steps) + at))
    for copy in firsts:
        copy.start()
    halo_copy = pltpu.make_async_remote_copy(
        src_ref=record,
        dst_ref=halo,
        send_sem=halo_sem.at[0],
        recv_sem=halo_sem.at[1],
        device_id={"tm": before},
        device_id_type=MESH,
    )
    halo_copy.start()
    own_pair = pair_copy(own, me, 0)
    own_pair.start()

    n_first = len(z_steps) + len(y_steps)

    @pl.when(core == 0)
    def _():
        at = n_first
        for back in [3, 1, 2]:
            owner = slot(at_y, (at_z + back) % ZRUN, core)
            piece_copy(bank.at[owner], owner, me, 0).wait_recv()
            for d in y_steps:
                target = slot((at_y + d) % rows_y, at_z, core)
                piece_copy(bank.at[owner], owner, target, at).start()
                at += 1

    @pl.when(core == 1)
    def _():
        at = n_first
        for back in [7, 1, 6, 2, 5, 3, 4]:
            owner = slot((at_y + back) % rows_y, at_z, core)
            piece_copy(bank.at[owner], owner, me, 0).wait_recv()
            for d in z_steps:
                target = slot(at_y, (at_z + d) % ZRUN, core)
                piece_copy(bank.at[owner], owner, target, at).start()
                at += 1

    halo_copy.wait_recv()
    for load in loads:
        load.wait()

    row16 = lax.broadcasted_iota(jnp.int32, (16, ext), 0)
    lag = jnp.zeros((16, ext), jnp.int32)
    for c in range(chans):
        lag = jnp.where(row16 == c, shift_s[c], lag)
    tail = jnp.where(me == count - 1, 0.0, halo[...].astype(jnp.float32))
    signal = jnp.concatenate([rec_buf[...].astype(jnp.float32), tail], axis=1)
    signal = jnp.concatenate([signal, jnp.zeros((16 - chans, ext), jnp.float32)], axis=0)
    for bit in range(8):
        signal = jnp.where(
            (lag & (1 << bit)) != 0, shifted_left(signal, 1 << bit), signal
        )
    signal = signal[:, :reach]
    aligned[...] = signal
    energy = signal * signal
    step = 1
    while step < taps:
        energy = energy + shifted_left(energy, step)
        step *= 2
    gain[...] = lax.rsqrt(energy[:, :span] + 1e-06)

    row8 = lax.broadcasted_iota(jnp.int32, (8, reach), 0)
    wide = span + taps // 2

    def build(c, carry):
        lanes = jnp.broadcast_to(aligned[pl.ds(c, 1), :], (8, reach))
        for bit in range(3):
            lanes = jnp.where((row8 & (1 << bit)) != 0, shifted_left(lanes, 1 << bit), lanes)
        for q in range(8):
            pair = jnp.concatenate(
                [shifted_left(lanes, 16 * q), shifted_left(lanes, 16 * q + 8)], axis=0
            ).astype(jnp.bfloat16)
            hankel[c, 16 * q : 16 * q + 16, :] = pair[:, :wide]
            hankel[c, 128 + 16 * q : 144 + 16 * q, :] = pair[:, 128 : 128 + wide]
        return carry

    lax.fori_loop(0, chans, build, 0)

    at = 1
    mine = []
    for dz in [0, 1, 3, 2]:
        for dy in [0, 7, 1, 6, 2, 5, 3, 4] if rows_y == 8 else range(rows_y):
            if dz or dy:
                mine.append(((at_z + dz) % ZRUN, (at_y + dy) % rows_y, dz == 0, dy == 0))
    for z, y, same_z, same_y in mine:
        owner = slot(y, z, core)
        relayed = jnp.where(core == 0, same_y, same_z)

        @pl.when(jnp.logical_not(relayed))
        def _():
            piece_copy(bank.at[owner], owner, me, 0).wait_recv()

        pair_copy(bank.at[owner], owner, at).start()
        at += 1

    for y in range(rows_y):
        for z in range(ZRUN):
            owner = slot(y, z, 1 - core)
            pair_copy(bank.at[owner], owner, 0).wait_recv()

    def widen(p, carry):
        piece = bank[plan_s[p]].astype(jnp.float32)
        for part in range(taps // 128):
            wave[part, pl.ds(pl.multiple_of(p * 16, 16), chans), :] = piece[
                :, part * 128 : part * 128 + 128
            ]
        return carry

    lax.fori_loop(0, count, widen, 0)

    overall = math.sqrt(taps / CHANNELS)
    total[...] = jnp.zeros_like(total)

    def channel(c, carry):
        panel = jnp.concatenate(
            [wave[part, pl.ds(c, count, stride=16), :] for part in range(taps // 128)], axis=1
        )
        norm = jnp.sum(panel * panel, axis=1, keepdims=True)
        weight = (live_s[c].astype(jnp.float32) * overall) * lax.rsqrt(norm + 1e-06)
        panel = panel.astype(jnp.bfloat16)
        corr = jnp.dot(
            panel[:, : taps // 2], hankel[c, :, :span], preferred_element_type=jnp.float32
        ) + jnp.dot(
            panel[:, taps // 2 :],
            hankel[c, :, taps // 2 : taps // 2 + span],
            preferred_element_type=jnp.float32,
        )
        total[...] += corr * weight * gain[pl.ds(c, 1), :]
        return carry

    lax.fori_loop(0, chans, channel, 0)

    per = count // (cols_x * ZHALVES)

    def block(h, x):
        return total.at[pl.ds(pl.multiple_of((h * cols_x + x) * per, per), per), :]

    def row_copy(far, d):
        h = 1 - half if far else half
        kind = 0 if far else 1
        return pltpu.make_async_remote_copy(
            src_ref=block(h, (at_x + d) % cols_x),
            dst_ref=row_recv.at[kind, d - 1],
            send_sem=row_ssem.at[kind, d - 1],
            recv_sem=row_rsem.at[kind, d - 1],
            device_id={"sta": half * cols_x + (at_x + d) % cols_x},
            device_id_type=MESH,
        )

    x_steps = [2, 1, 3] if cols_x == 4 else list(range(1, cols_x))
    row_copies = [row_copy(far, d) for far in (True, False) for d in x_steps]
    for copy in row_copies:
        copy.start()
    for copy in row_copies[: len(x_steps)]:
        copy.wait_recv()
    far_send[...] = block(1 - half, at_x)[...] + sum(
        row_recv[0, d - 1] for d in range(1, cols_x)
    )
    far_copy = pltpu.make_async_remote_copy(
        src_ref=far_send,
        dst_ref=far_recv,
        send_sem=far_sem.at[0],
        recv_sem=far_sem.at[1],
        device_id={"sta": far_peer},
        device_id_type=MESH,
    )
    far_copy.start()
    for copy in row_copies[len(x_steps) :]:
        copy.wait_recv()
    near = block(half, at_x)[...] + sum(row_recv[1, d - 1] for d in range(1, cols_x))
    far_copy.wait_recv()
    out[...] = near + far_recv[...]

    for copy in row_copies + [far_copy, halo_copy]:
        copy.wait_send()
    for at in range(n_first + 21 if rows_y == 8 else n_first):
        piece_copy(own, me, me, at).wait_send()
    for at in range(rows_y * ZRUN):
        pair_copy(own, me, at).wait_send()


def per_device(rows_y, cols_x, record, templates, shifts, live, plan):
    chans, span = record.shape
    taps = templates.shape[2]
    count = plan.shape[0]
    per = count // (cols_x * ZHALVES)
    any_spec = pl.BlockSpec(memory_space=pl.ANY)
    dma = pltpu.SemaphoreType.DMA
    pieces = rows_y * ZRUN
    return pl.pallas_call(
        functools.partial(stack_kernel, (rows_y, cols_x, chans, span, taps)),
        out_shape=jax.ShapeDtypeStruct((per, span), jnp.float32),
        in_specs=[any_spec] * 5,
        out_specs=pl.BlockSpec(memory_space=pltpu.VMEM),
        scratch_shapes=[
            pltpu.VMEM((chans, span), jnp.bfloat16),
            pltpu.VMEM((chans, span), jnp.bfloat16),
            pltpu.VMEM((count, chans, taps), jnp.bfloat16),
            pltpu.VMEM((taps // 128, count * 16, 128), jnp.float32),
            pltpu.VMEM((chans, taps // 2, span + taps // 2), jnp.bfloat16),
            pltpu.VMEM((16, span), jnp.float32),
            pltpu.VMEM((16, span + taps), jnp.float32),
            pltpu.VMEM((count, span), jnp.float32),
            pltpu.VMEM((2, cols_x - 1, per, span), jnp.float32),
            pltpu.VMEM((per, span), jnp.float32),
            pltpu.VMEM((per, span), jnp.float32),
            pltpu.SMEM(shifts.shape, jnp.int32),
            pltpu.SMEM(live.shape, jnp.int32),
            pltpu.SMEM(plan.shape, jnp.int32),
            dma((5,)),
            dma((2,)),
            dma((pieces - 1,)),
            dma((count,)),
            dma((pieces,)),
            dma((count,)),
            dma((2, cols_x - 1)),
            dma((2, cols_x - 1)),
            dma((2,)),
        ],
        compiler_params=pltpu.CompilerParams(
            collective_id=0, has_side_effects=True, vmem_limit_bytes=40 * 2**20
        ),
    )(record, templates, shifts, live, plan)


def solution(mesh):
    cols_x = mesh.shape["sta"] // ZHALVES
    rows_y = mesh.shape["tm"] // (2 * ZRUN)
    placed = (P("sta", "tm"), P("tm", "sta", None), P("sta"), P("sta"), P())
    return jax.shard_map(
        functools.partial(per_device, rows_y, cols_x),
        mesh=mesh,
        in_specs=placed,
        out_specs=P("sta", "tm"),
        check_vma=False,
    )
```

time: 319 us -> 45.5 us (0.14)
  local copies, waits for them, and re-layouts: 111 us -> 4.03 us
  waiting for transfers between devices: 86.1 us -> 0 us
  blocking collectives: 80.2 us -> 0 us
  Pallas kernels: 0 us -> 41.2 us
  matrix products: 13.6 us -> 0 us
  between operations: 13.5 us -> 0.01 us
  starting transfers between devices: 8.87 us -> 0 us
  other arithmetic: 3.33 us -> 0 us
    reduce_scatter x1 -> x0, waiting for transfers between devices: 86.1 us -> none  [per_device(): lax.psum_scatter(partial_value, 'sta', scatter_dimension=0, tiled=True)]
    all_gather x1 -> x0, blocking collectives: 80.2 us -> none  [per_device(): bank_all = lax.all_gather(templates, 'tm', axis=0, tiled=True)]
    reshape x3 -> x0, local copies, waits for them, and re-layouts: 44.7 us -> none  [hankel_rows(): skewed = copies[:taps_len * (length + 1)].reshape(taps_len, length + 1)]
    pallas_call x0 -> x1, Pallas kernels: none -> 41.2 us  [per_device(): pl.pallas_call(functools.partial(stack_kernel, (rows_y, cols_x, chans, sp...]
    while x9 -> x0, local copies, waits for them, and re-layouts: 27.6 us -> none
    gather x49 -> x0, local copies, waits for them, and re-layouts: 25.4 us -> none
    dot_general x6 -> x0, matrix products: 13.6 us -> none  [the longest x3 7.72 us: add_group(): jnp.einsum('rgl,glt->rgt', panel_part, stacked, preferred_element_type=jn...]
    slice x3 -> x0, local copies, waits for them, and re-layouts: 12 us -> none  [hankel_rows(): skewed = copies[:taps_len * (length + 1)].reshape(taps_len, length + 1)]
  transfers between devices with their start and end apart: 2 -> 0, of which waited for: 1 -> 0; matrix products, arithmetic and copies ran while one was open for 1% -> 0% of each run, Pallas kernels for 0% -> 0%
where the time goes in v1:
time: 45.5 us; the launch traced here: 45.3 us
  Pallas kernels  41.2 us (91%)
  local copies, waits for them, and re-layouts  4.03 us (9%)
    pallas_call x1, Pallas kernels, per_device(): pl.pallas_call(functools.partial(stack_kernel, (rows_y, cols_x, chans, sp...  41.2 us
    unnamed x11, local copies, waits for them, and re-layouts  4.03 us

profile of v1, /device:TPU:1, one launch (start us, length us, event | category | flops | bytes accessed | tf_op | source)
XLA Modules:
  0.0 45.3 jit_solution(7603420731590428591)
XLA Ops:
  0.0 0.0 copy-start
  0.0 0.7 %copy-done = bf16[12,768]{1,0:T(8,128)(2,1)S(1)} copy-done((bf16[12,768]{1,0:T(8,128)(2,1)S(1)}, bf16[12,768]{1,0:T(8,128)(2,1)}, u32[]{:S(2)}) %copy-start) | copy-done | bytes 18456
  0.7 0.0 copy-start.1
  0.7 0.7 %copy-done.1 = bf16[1,12,512]{2,1,0:T(8,128)(2,1)S(1)} copy-done((bf16[1,12,512]{2,1,0:T(8,128)(2,1)S(1)}, bf16[1,12,512]{2,1,0:T(8,128)(2,1)}, u32[]{:S(2)}) %copy-start.1) | copy-done | bytes 12312
  1.5 0.0 copy-start.2
  1.5 0.7 %copy-done.2 = s32[12]{0:T(128)S(1)} copy-done((s32[12]{0:T(128)S(1)}, s32[12]{0:T(128)}, u32[]{:S(2)}) %copy-start.2) | copy-done | bytes 72
  2.1 0.0 copy-start.3
  2.1 0.7 %copy-done.3 = s32[12]{0:T(128)S(1)} copy-done((s32[12]{0:T(128)S(1)}, s32[12]{0:T(128)}, u32[]{:S(2)}) %copy-start.3) | copy-done | bytes 72
  2.8 0.0 copy-start.4
  2.8 0.7 %copy-done.4 = s32[64]{0:T(128)S(1)} copy-done((s32[64]{0:T(128)S(1)}, s32[64]{0:T(128)}, u32[]{:S(2)}) %copy-start.4) | copy-done | bytes 280
  3.4 41.2 %shard_map.55 = f32[8,768]{1,0:T(8,128)S(1)} custom-call(bf16[12,768]{1,0:T(8,128)(2,1)S(1)} %copy-done, bf16[1,12,512]{2,1,0:T(8,128)(2,1)S(1)} %copy-done.1, s32[12]{0:T(128)S(1)} %copy-done.2, s32[12]{0:T(128)S(1)} %copy-done.3, s32[64]{0:T(128)S(1)} %copy-done.4), custom_call_target="tpu_custom_call" | custom-call | tf_op jit(solution)/shard_map/pallas_call | solution.py:314
  44.7 0.6 %copy.7 = f32[8,768]{1,0:T(8,128)} copy(f32[8,768]{1,0:T(8,128)S(1)} %shard_map.55) | data formatting | bytes 49152
Async XLA Ops:
  0.0 0.7 %copy-start = (bf16[12,768]{1,0:T(8,128)(2,1)S(1)}, bf16[12,768]{1,0:T(8,128)(2,1)}, u32[]{:S(2)}) copy-start(bf16[12,768]{1,0:T(8,128)(2,1)} %record.1) | copy-start | bytes 55300
  0.7 0.7 %copy-start.1 = (bf16[1,12,512]{2,1,0:T(8,128)(2,1)S(1)}, bf16[1,12,512]{2,1,0:T(8,128)(2,1)}, u32[]{:S(2)}) copy-start(bf16[1,12,512]{2,1,0:T(8,128)(2,1)} %templates.1) | copy-start | bytes 36868
  1.5 0.7 %copy-start.2 = (s32[12]{0:T(128)S(1)}, s32[12]{0:T(128)}, u32[]{:S(2)}) copy-start(s32[12]{0:T(128)} %shifts.1) | copy-start | bytes 148
  2.1 0.7 %copy-start.3 = (s32[12]{0:T(128)S(1)}, s32[12]{0:T(128)}, u32[]{:S(2)}) copy-start(s32[12]{0:T(128)} %live.1) | copy-start | bytes 148
  2.8 0.7 %copy-start.4 = (s32[64]{0:T(128)S(1)}, s32[64]{0:T(128)}, u32[]{:S(2)}) copy-start(s32[64]{0:T(128)} %plan.1) | copy-start | bytes 772

commit v2 on v1

v2 whole, which is shorter than its diff:
```python
import functools
import math

import jax
import jax.numpy as jnp
from jax import lax
from jax.experimental import pallas as pl
from jax.experimental.pallas import tpu as pltpu
from jax.sharding import PartitionSpec as P

CHANNELS = 96
ZRUN = 4
ZHALVES = 2
MESH = pl.DeviceIdType.MESH


def shifted_left(value, by):
    width = value.shape[1]
    if by % width == 0:
        return value
    return pltpu.roll(value, width - by, 1)


def stack_kernel(
    sizes,
    record,
    templates,
    shifts,
    live,
    plan,
    out,
    rec_buf,
    halo,
    bank,
    wave,
    hankel,
    gain,
    aligned,
    total,
    row_recv,
    shift_s,
    live_s,
    plan_s,
    load_sem,
    halo_sem,
    send_sem,
    recv_sem,
    pair_sem,
    row_ssem,
    row_rsem,
):
    rows_y, cols_x, chans, span, taps = sizes
    count = rows_y * ZRUN * 2
    ext = 2 * span
    reach = span + taps
    sta = lax.axis_index("sta")
    me = lax.axis_index("tm")
    core = me % 2
    at_z = (me // 2) % ZRUN
    at_y = me // (2 * ZRUN)
    at_x = sta % cols_x
    half = sta // cols_x

    def slot(y, z, c):
        return (y * ZRUN + z) * 2 + c

    def place(y, z, c):
        return (c * rows_y + y) * ZRUN + z

    after, before = (me + 1) % count, (me + count - 1) % count
    partner = slot(at_y, at_z, 1 - core)
    y_peers = [slot((at_y + d) % rows_y, at_z, core) for d in range(1, rows_y)]
    z_peers = [slot(at_y, (at_z + d) % ZRUN, core) for d in range(1, ZRUN)]
    x_peers = [half * cols_x + (at_x + d) % cols_x for d in range(1, cols_x)]
    far_peers = [(1 - half) * cols_x + (at_x + d) % cols_x for d in range(cols_x)]
    outer = jnp.where(core == 0, before, after)

    barrier = pltpu.get_barrier_semaphore()
    met = [{"sta": p} for p in x_peers + far_peers]
    met += [{"tm": p} for p in y_peers + z_peers + [partner, outer]]
    for peer in met:
        pl.semaphore_signal(barrier, inc=1, device_id=peer, device_id_type=MESH)

    mine = place(at_y, at_z, core)
    loads = [
        pltpu.make_async_copy(record, rec_buf, load_sem.at[0]),
        pltpu.make_async_copy(templates.at[0], bank.at[mine], load_sem.at[1]),
        pltpu.make_async_copy(shifts, shift_s, load_sem.at[2]),
        pltpu.make_async_copy(live, live_s, load_sem.at[3]),
        pltpu.make_async_copy(plan, plan_s, load_sem.at[4]),
    ]
    for load in loads:
        load.start()

    pl.semaphore_wait(barrier, len(met))

    def piece_copy(src, index, sem, target):
        return pltpu.make_async_remote_copy(
            src_ref=src,
            dst_ref=bank.at[index],
            send_sem=send_sem.at[0],
            recv_sem=recv_sem.at[sem],
            device_id={"tm": target},
            device_id_type=MESH,
        )

    def group_wait(y, first, size, sem):
        group = bank.at[pl.ds(first, size)]
        pltpu.make_async_remote_copy(
            src_ref=group,
            dst_ref=group,
            send_sem=send_sem.at[0],
            recv_sem=recv_sem.at[sem],
            device_id={"tm": me},
            device_id_type=MESH,
        ).wait_recv()

    own = templates.at[0]
    z_steps = list(range(1, ZRUN))
    y_steps = sorted(range(1, rows_y), key=lambda d: -min(d, rows_y - d))
    z_sem = jnp.where(core == 0, at_z, rows_y + at_y)
    y_sem = jnp.where(core == 0, rows_y + at_y, at_y)

    def own_to_z():
        for d in z_steps:
            piece_copy(own, mine, z_sem, slot(at_y, (at_z + d) % ZRUN, core)).start()

    def own_to_y():
        for d in y_steps:
            piece_copy(own, mine, y_sem, slot((at_y + d) % rows_y, at_z, core)).start()

    @pl.when(core == 0)
    def _():
        own_to_z()
        own_to_y()

    @pl.when(core == 1)
    def _():
        own_to_y()
        own_to_z()

    halo_copy = pltpu.make_async_remote_copy(
        src_ref=record,
        dst_ref=halo,
        send_sem=halo_sem.at[0],
        recv_sem=halo_sem.at[1],
        device_id={"tm": before},
        device_id_type=MESH,
    )
    halo_copy.start()

    @pl.when(core == 0)
    def _():
        for back in [3, 1, 2]:
            z = (at_z + back) % ZRUN
            index = place(at_y, z, core)
            piece_copy(bank.at[index], index, z, me).wait_recv()
            for d in y_steps:
                target = slot((at_y + d) % rows_y, at_z, core)
                piece_copy(bank.at[index], index, rows_y + at_y, target).start()

    @pl.when(core == 1)
    def _():
        for back in y_steps[::-1]:
            y = (at_y + back) % rows_y
            index = place(y, at_z, core)
            piece_copy(bank.at[index], index, y, me).wait_recv()
            for d in z_steps:
                target = slot(at_y, (at_z + d) % ZRUN, core)
                piece_copy(bank.at[index], index, rows_y + y, target).start()

    halo_copy.wait_recv()
    for load in loads:
        load.wait()

    row16 = lax.broadcasted_iota(jnp.int32, (16, ext), 0)
    lag = jnp.zeros((16, ext), jnp.int32)
    for c in range(chans):
        lag = jnp.where(row16 == c, shift_s[c], lag)
    tail = jnp.where(me == count - 1, 0.0, halo[...].astype(jnp.float32))
    signal = jnp.concatenate([rec_buf[...].astype(jnp.float32), tail], axis=1)
    signal = jnp.concatenate([signal, jnp.zeros((16 - chans, ext), jnp.float32)], axis=0)
    for bit in range(8):
        signal = jnp.where(
            (lag & (1 << bit)) != 0, shifted_left(signal, 1 << bit), signal
        )
    signal = signal[:, :reach]
    aligned[...] = signal
    energy = signal * signal
    step = 1
    while step < taps:
        energy = energy + shifted_left(energy, step)
        step *= 2
    gain[...] = lax.rsqrt(energy[:, :span] + 1e-06)

    row8 = lax.broadcasted_iota(jnp.int32, (8, reach), 0)
    wide = span + taps // 2

    def build(c, carry):
        lanes = jnp.broadcast_to(aligned[pl.ds(c, 1), :], (8, reach))
        for bit in range(3):
            lanes = jnp.where((row8 & (1 << bit)) != 0, shifted_left(lanes, 1 << bit), lanes)
        for q in range(8):
            pair = jnp.concatenate(
                [shifted_left(lanes, 16 * q), shifted_left(lanes, 16 * q + 8)], axis=0
            ).astype(jnp.bfloat16)
            hankel[c, 16 * q : 16 * q + 16, :] = pair[:, :wide]
            hankel[c, 128 + 16 * q : 144 + 16 * q, :] = pair[:, 128 : 128 + wide]
        return carry

    lax.fori_loop(0, chans, build, 0)

    def hand_over(y):
        group = bank.at[pl.ds(place(y, 0, core), ZRUN)]
        pltpu.make_async_remote_copy(
            src_ref=group,
            dst_ref=group,
            send_sem=pair_sem.at[0],
            recv_sem=pair_sem.at[1],
            device_id={"tm": partner},
            device_id_type=MESH,
        ).start()

    for d in [0] + y_steps[::-1]:
        y = (at_y + d) % rows_y
        base = place(y, 0, core)
        if d:

            @pl.when(core == 0)
            def _():
                group_wait(y, base, ZRUN, rows_y + y)

        @pl.when(core == 1)
        def _():
            group_wait(y, base, ZRUN - 1, rows_y + y)

        hand_over(y)

    pieces = rows_y * ZRUN
    theirs = bank.at[pl.ds((1 - core) * pieces, pieces)]
    handed = pltpu.make_async_remote_copy(
        src_ref=theirs,
        dst_ref=theirs,
        send_sem=pair_sem.at[0],
        recv_sem=pair_sem.at[1],
        device_id={"tm": me},
        device_id_type=MESH,
    )
    handed.wait_recv()

    def widen(p, carry):
        piece = bank[(plan_s[p] % 2) * pieces + plan_s[p] // 2].astype(jnp.float32)
        for part in range(taps // 128):
            wave[part, pl.ds(pl.multiple_of(p * 16, 16), chans), :] = piece[
                :, part * 128 : part * 128 + 128
            ]
        return carry

    overall = math.sqrt(taps / CHANNELS)
    some = count // ZHALVES

    def stack(first):
        lax.fori_loop(0, some, lambda i, carry: widen(first + i, carry), 0, unroll=4)
        running = jnp.zeros((some, span), jnp.float32)
        for c in range(chans):
            panel = jnp.concatenate(
                [wave[part, pl.ds(first * 16 + c, some, stride=16), :] for part in range(taps // 128)],
                axis=1,
            )
            norm = jnp.sum(panel * panel, axis=1, keepdims=True)
            weight = (live_s[c].astype(jnp.float32) * overall) * lax.rsqrt(norm + 1e-06)
            panel = panel.astype(jnp.bfloat16)
            half_taps = taps // 2
            both = jnp.concatenate([panel[:, :half_taps], panel[:, half_taps:]], axis=0)
            tiles = span // half_taps
            parts = []
            for t in range(tiles + 1):
                rows = both[:some] if t == 0 else both[some:] if t == tiles else both
                parts.append(
                    jnp.dot(
                        rows,
                        hankel[c, :, t * half_taps : (t + 1) * half_taps],
                        preferred_element_type=jnp.float32,
                    )
                )
            corr = jnp.concatenate(
                [parts[t][:some] + parts[t + 1][-some:] for t in range(tiles)], axis=1
            )
            running = running + corr * weight * gain[c : c + 1, :]
        total[pl.ds(pl.multiple_of(first, some), some), :] = running

    per = count // (cols_x * ZHALVES)

    def block(h, x):
        return total.at[pl.ds(pl.multiple_of((h * cols_x + x) * per, per), per), :]

    def row_copy(far, d):
        h = 1 - half if far else half
        kind = 0 if far else 1
        return pltpu.make_async_remote_copy(
            src_ref=block(h, (at_x + d) % cols_x),
            dst_ref=row_recv.at[kind, d],
            send_sem=row_ssem.at[kind, d],
            recv_sem=row_rsem.at[kind, d],
            device_id={"sta": h * cols_x + (at_x + d) % cols_x},
            device_id_type=MESH,
        )

    x_steps = [2, 1, 3, 0] if cols_x == 4 else list(range(cols_x))
    stack((1 - half) * some)
    far_copies = [row_copy(True, d) for d in x_steps]
    for copy in far_copies:
        copy.start()
    stack(half * some)
    near_copies = [row_copy(False, d) for d in x_steps if d]
    for copy in near_copies:
        copy.start()
    sent = bank.at[pl.ds(0, pieces - 1)]
    pltpu.make_async_remote_copy(
        src_ref=sent,
        dst_ref=sent,
        send_sem=send_sem.at[0],
        recv_sem=recv_sem.at[0],
        device_id={"tm": me},
        device_id_type=MESH,
    ).wait_send()
    handed.wait_send()
    halo_copy.wait_send()
    for copy in near_copies:
        copy.wait_recv()
    near = block(half, at_x)[...] + sum(row_recv[1, d] for d in range(1, cols_x))
    for copy in far_copies:
        copy.wait_recv()
    out[...] = near + sum(row_recv[0, d] for d in range(cols_x))
    for copy in far_copies + near_copies:
        copy.wait_send()


def per_device(rows_y, cols_x, record, templates, shifts, live, plan):
    chans, span = record.shape
    taps = templates.shape[2]
    count = plan.shape[0]
    per = count // (cols_x * ZHALVES)
    any_spec = pl.BlockSpec(memory_space=pl.ANY)
    dma = pltpu.SemaphoreType.DMA
    return pl.pallas_call(
        functools.partial(stack_kernel, (rows_y, cols_x, chans, span, taps)),
        out_shape=jax.ShapeDtypeStruct((per, span), jnp.float32),
        in_specs=[any_spec] * 5,
        out_specs=pl.BlockSpec(memory_space=pltpu.VMEM),
        scratch_shapes=[
            pltpu.VMEM((chans, span), jnp.bfloat16),
            pltpu.VMEM((chans, span), jnp.bfloat16),
            pltpu.VMEM((count, chans, taps), jnp.bfloat16),
            pltpu.VMEM((taps // 128, count * 16, 128), jnp.float32),
            pltpu.VMEM((chans, taps // 2, span + taps // 2), jnp.bfloat16),
            pltpu.VMEM((16, span), jnp.float32),
            pltpu.VMEM((16, span + taps), jnp.float32),
            pltpu.VMEM((count, span), jnp.float32),
            pltpu.VMEM((2, cols_x, per, span), jnp.float32),
            pltpu.SMEM(shifts.shape, jnp.int32),
            pltpu.SMEM(live.shape, jnp.int32),
            pltpu.SMEM(plan.shape, jnp.int32),
            dma((5,)),
            dma((2,)),
            dma((1,)),
            dma((2 * rows_y,)),
            dma((2,)),
            dma((2, cols_x)),
            dma((2, cols_x)),
        ],
        compiler_params=pltpu.CompilerParams(
            collective_id=0, has_side_effects=True, vmem_limit_bytes=67043328
        ),
    )(record, templates, shifts, live, plan)


def solution(mesh):
    cols_x = mesh.shape["sta"] // ZHALVES
    rows_y = mesh.shape["tm"] // (2 * ZRUN)
    placed = (P("sta", "tm"), P("tm", "sta", None), P("sta"), P("sta"), P())
    return jax.shard_map(
        functools.partial(per_device, rows_y, cols_x),
        mesh=mesh,
        in_specs=placed,
        out_specs=P("sta", "tm"),
        check_vma=False,
    )
```

time: 45.5 us -> 39.3 us (0.86)
  Pallas kernels: 41.2 us -> 37.7 us
  local copies, waits for them, and re-layouts: 4.03 us -> 1.35 us
    pallas_call x1, Pallas kernels: 41.2 us -> 37.7 us  [per_device(): pl.pallas_call(functools.partial(stack_kernel, (rows_y, cols_x, chans, sp...]
    unnamed x11 -> x1, local copies, waits for them, and re-layouts: 4.03 us -> 1.35 us
where the time goes in v2:
time: 39.3 us; the launch traced here: 39.1 us
  Pallas kernels  37.7 us (96%)
  local copies, waits for them, and re-layouts  1.35 us (3%)
    pallas_call x1, Pallas kernels, per_device(): pl.pallas_call(functools.partial(stack_kernel, (rows_y, cols_x, chans, sp...  37.7 us
    unnamed x1, local copies, waits for them, and re-layouts  1.35 us

profile of v2, /device:TPU:1, one launch (start us, length us, event | category | flops | bytes accessed | tf_op | source)
XLA Modules:
  0.0 39.1 jit_solution(17915463181438425682)
XLA Ops:
  0.0 37.7 %shard_map.55 = f32[8,768]{1,0:T(8,128)} custom-call(bf16[12,768]{1,0:T(8,128)(2,1)} %record.1, bf16[1,12,512]{2,1,0:T(8,128)(2,1)} %templates.1, s32[12]{0:T(128)} %shifts.1, s32[12]{0:T(128)} %live.1, s32[64]{0:T(128)} %plan.1), custom_call_target="tpu_custom_call" | custom-call | tf_op jit(solution)/shard_map/pallas_call | solution.py:346
  37.8 1.3 %copy.7 = f32[8,768]{1,0:T(8,128)} copy(f32[8,768]{1,0:T(8,128)} %shard_map.55) | data formatting | bytes 49152

commit v3 on v2

--- a/solution.py
+++ b/solution.py
@@ -11,6 +11,7 @@
 CHANNELS = 96
 ZRUN = 4
 ZHALVES = 2
+Z_ORDER = (1, 3, 2)
 MESH = pl.DeviceIdType.MESH
 
 
@@ -33,6 +34,7 @@
     halo,
     bank,
     wave,
+    weights,
     hankel,
     gain,
     aligned,
@@ -118,26 +120,30 @@
     own = templates.at[0]
     z_steps = list(range(1, ZRUN))
     y_steps = sorted(range(1, rows_y), key=lambda d: -min(d, rows_y - d))
-    z_sem = jnp.where(core == 0, at_z, rows_y + at_y)
-    y_sem = jnp.where(core == 0, rows_y + at_y, at_y)
-
-    def own_to_z():
-        for d in z_steps:
-            piece_copy(own, mine, z_sem, slot(at_y, (at_z + d) % ZRUN, core)).start()
-
-    def own_to_y():
-        for d in y_steps:
-            piece_copy(own, mine, y_sem, slot((at_y + d) % rows_y, at_z, core)).start()
-
-    @pl.when(core == 0)
-    def _():
-        own_to_z()
-        own_to_y()
-
-    @pl.when(core == 1)
-    def _():
-        own_to_y()
-        own_to_z()
+    y_far = [d for d in y_steps if min(d, rows_y - d) > 2]
+    y_near = [d for d in y_steps if min(d, rows_y - d) <= 2]
+
+    def z_sem(z):
+        return z
+
+    def far_sem(y):
+        return ZRUN + y
+
+    def group_sem(y):
+        return ZRUN + rows_y + y
+
+    def to_y(d):
+        return slot((at_y + d) % rows_y, at_z, core)
+
+    def to_z(d):
+        return slot(at_y, (at_z + d) % ZRUN, core)
+
+    for d in y_far:
+        piece_copy(own, mine, far_sem(at_y), to_y(d)).start()
+    for d in z_steps:
+        piece_copy(own, mine, z_sem(at_z), to_z(d)).start()
+    for d in y_near:
+        piece_copy(own, mine, group_sem(at_y), to_y(d)).start()
 
     halo_copy = pltpu.make_async_remote_copy(
         src_ref=record,
@@ -149,25 +155,18 @@
     )
     halo_copy.start()
 
-    @pl.when(core == 0)
-    def _():
-        for back in [3, 1, 2]:
-            z = (at_z + back) % ZRUN
-            index = place(at_y, z, core)
-            piece_copy(bank.at[index], index, z, me).wait_recv()
-            for d in y_steps:
-                target = slot((at_y + d) % rows_y, at_z, core)
-                piece_copy(bank.at[index], index, rows_y + at_y, target).start()
-
-    @pl.when(core == 1)
-    def _():
-        for back in y_steps[::-1]:
-            y = (at_y + back) % rows_y
-            index = place(y, at_z, core)
-            piece_copy(bank.at[index], index, y, me).wait_recv()
-            for d in z_steps:
-                target = slot(at_y, (at_z + d) % ZRUN, core)
-                piece_copy(bank.at[index], index, rows_y + y, target).start()
+    for back in Z_ORDER:
+        z = (at_z + back) % ZRUN
+        index = place(at_y, z, core)
+        piece_copy(bank.at[index], index, z_sem(z), me).wait_recv()
+        for d in y_near:
+            piece_copy(bank.at[index], index, group_sem(at_y), to_y(d)).start()
+    for back in y_far[::-1]:
+        y = (at_y + back) % rows_y
+        index = place(y, at_z, core)
+        piece_copy(bank.at[index], index, far_sem(y), me).wait_recv()
+        for d in z_steps:
+            piece_copy(bank.at[index], index, group_sem(y), to_z(d)).start()
 
     halo_copy.wait_recv()
     for load in loads:
@@ -200,15 +199,14 @@
         lanes = jnp.broadcast_to(aligned[pl.ds(c, 1), :], (8, reach))
         for bit in range(3):
             lanes = jnp.where((row8 & (1 << bit)) != 0, shifted_left(lanes, 1 << bit), lanes)
+        lanes = jnp.concatenate([lanes, shifted_left(lanes, 8)], axis=0).astype(jnp.bfloat16)
         for q in range(8):
-            pair = jnp.concatenate(
-                [shifted_left(lanes, 16 * q), shifted_left(lanes, 16 * q + 8)], axis=0
-            ).astype(jnp.bfloat16)
+            pair = shifted_left(lanes, 16 * q)
             hankel[c, 16 * q : 16 * q + 16, :] = pair[:, :wide]
             hankel[c, 128 + 16 * q : 144 + 16 * q, :] = pair[:, 128 : 128 + wide]
         return carry
 
-    lax.fori_loop(0, chans, build, 0)
+    lax.fori_loop(0, chans, build, 0, unroll=2)
 
     def hand_over(y):
         group = bank.at[pl.ds(place(y, 0, core), ZRUN)]
@@ -224,16 +222,10 @@
     for d in [0] + y_steps[::-1]:
         y = (at_y + d) % rows_y
         base = place(y, 0, core)
-        if d:
-
-            @pl.when(core == 0)
-            def _():
-                group_wait(y, base, ZRUN, rows_y + y)
-
-        @pl.when(core == 1)
-        def _():
-            group_wait(y, base, ZRUN - 1, rows_y + y)
-
+        if d in y_near:
+            group_wait(y, base, ZRUN, group_sem(y))
+        elif d:
+            group_wait(y, base, ZRUN - 1, group_sem(y))
         hand_over(y)
 
     pieces = rows_y * ZRUN
@@ -248,27 +240,36 @@
     )
     handed.wait_recv()
 
+    overall = math.sqrt(taps / CHANNELS)
+    row12 = lax.broadcasted_iota(jnp.int32, (chans, 1), 0)
+    live_col = jnp.zeros((chans, 1), jnp.float32)
+    for c in range(chans):
+        live_col = jnp.where(row12 == c, live_s[c].astype(jnp.float32) * overall, live_col)
+
     def widen(p, carry):
         piece = bank[(plan_s[p] % 2) * pieces + plan_s[p] // 2].astype(jnp.float32)
         for part in range(taps // 128):
             wave[part, pl.ds(pl.multiple_of(p * 16, 16), chans), :] = piece[
                 :, part * 128 : part * 128 + 128
             ]
+        norm = jnp.sum(piece * piece, axis=1, keepdims=True)
+        scale = live_col * lax.rsqrt(norm + 1e-06)
+        weights[pl.ds(pl.multiple_of(p * 16, 16), chans), :] = jnp.broadcast_to(scale, (chans, 128))
         return carry
 
     overall = math.sqrt(taps / CHANNELS)
     some = count // ZHALVES
 
     def stack(first):
-        lax.fori_loop(0, some, lambda i, carry: widen(first + i, carry), 0, unroll=4)
+        lax.fori_loop(0, some, lambda i, carry: widen(first + i, carry), 0, unroll=16)
         running = jnp.zeros((some, span), jnp.float32)
         for c in range(chans):
             panel = jnp.concatenate(
                 [wave[part, pl.ds(first * 16 + c, some, stride=16), :] for part in range(taps // 128)],
                 axis=1,
             )
-            norm = jnp.sum(panel * panel, axis=1, keepdims=True)
-            weight = (live_s[c].astype(jnp.float32) * overall) * lax.rsqrt(norm + 1e-06)
+            weight = weights[pl.ds(first * 16 + c, some, stride=16), :]
+            weight = jnp.concatenate([weight] * (span // 128), axis=1)
             panel = panel.astype(jnp.bfloat16)
             half_taps = taps // 2
             both = jnp.concatenate([panel[:, :half_taps], panel[:, half_taps:]], axis=0)
@@ -353,6 +354,7 @@
             pltpu.VMEM((chans, span), jnp.bfloat16),
             pltpu.VMEM((count, chans, taps), jnp.bfloat16),
             pltpu.VMEM((taps // 128, count * 16, 128), jnp.float32),
+            pltpu.VMEM((count * 16, 128), jnp.float32),
             pltpu.VMEM((chans, taps // 2, span + taps // 2), jnp.bfloat16),
             pltpu.VMEM((16, span), jnp.float32),
             pltpu.VMEM((16, span + taps), jnp.float32),
@@ -364,7 +366,7 @@
             dma((5,)),
             dma((2,)),
             dma((1,)),
-            dma((2 * rows_y,)),
+            dma((ZRUN + 2 * rows_y,)),
             dma((2,)),
             dma((2, cols_x)),
             dma((2, cols_x)),

time: 39.3 us -> 37.1 us (0.944)
  Pallas kernels: 37.7 us -> 35.6 us
    pallas_call x1, Pallas kernels: 37.7 us -> 35.6 us  [per_device(): pl.pallas_call(functools.partial(stack_kernel, (rows_y, cols_x, chans, sp...]
where the time goes in v3:
time: 37.1 us; the launch traced here: 36.9 us
  Pallas kernels  35.6 us (96%)
  local copies, waits for them, and re-layouts  1.35 us (4%)
    pallas_call x1, Pallas kernels, per_device(): pl.pallas_call(functools.partial(stack_kernel, (rows_y, cols_x, chans, sp...  35.6 us
    unnamed x1, local copies, waits for them, and re-layouts  1.35 us

profile of v3, /device:TPU:1, one launch (start us, length us, event | category | flops | bytes accessed | tf_op | source)
XLA Modules:
  0.0 36.9 jit_solution(5050065300281495317)
XLA Ops:
  0.0 35.6 %shard_map.55 = f32[8,768]{1,0:T(8,128)} custom-call(bf16[12,768]{1,0:T(8,128)(2,1)} %record.1, bf16[1,12,512]{2,1,0:T(8,128)(2,1)} %templates.1, s32[12]{0:T(128)} %shifts.1, s32[12]{0:T(128)} %live.1, s32[64]{0:T(128)} %plan.1), custom_call_target="tpu_custom_call" | custom-call | tf_op jit(solution)/shard_map/pallas_call | solution.py:347
  35.6 1.3 %copy.7 = f32[8,768]{1,0:T(8,128)} copy(f32[8,768]{1,0:T(8,128)} %shard_map.55) | data formatting | bytes 49152
